TPU v7x, 256 devices: a whole 4x4x8 slice. The times are simulated.
256 devices in a mesh: row: 16 (over y, x), col: 16 (over z, core).
Axes of the slice: x: 4, y: 4, z: 8, core: 2. Of those that a mesh axis runs over, the one named last changes fastest.
Arguments:
- trail_grad: float32 [16384, 16384], P('row', 'col'), may hold values from -20 to 20, as said below
- factor_rows: float32 [16384, 768], P('col', 'row'), may hold values from -0.046875 to 0.046875
- factor_top: float32 [768, 768], replicated, may hold values from -1 to 2, as said below
- rows_grad: float32 [16384, 768], P(('row', 'col')), may hold values from -6 to 6
- top_grad: float32 [768, 768], replicated, may hold values from -6 to 6, as said below
Outputs:
- rows_adjoint: float32 [16384, 768], P(('row', 'col'))
- top_adjoint: float32 [768, 768], replicated
Inputs may be any that keep to these rules, and one draw needn't show every extreme that they name: trail_grad is symmetric once both of its orders are reverted. factor_top is lower triangular with its diagonal between 1 and 2. top_grad is lower triangular.
All inputs are finite; a program needn't handle non-finite values.
Results may differ from a plain program's by a relative error of at most 0.0001.
Values sent between devices are 32-bit elements; how exact they have to be, the bound alone decides.
A program may use at most 64 MiB of HBM per device.

v0:
```python
import jax
import jax.numpy as jnp
from jax import lax
from jax.sharding import PartitionSpec as P

NB = 256
NP = 3
CB = 128
exact_dots = lax.Precision.HIGHEST


def product(left, right):
    return jnp.dot(left, right, precision=exact_dots, preferred_element_type=jnp.float32)


def column_products(left, right):
    return jnp.einsum(
        "ia,ib->ab", left, right, precision=exact_dots, preferred_element_type=jnp.float32
    )


def halve_diagonal(matrix):
    order = matrix.shape[0]
    row_ids = lax.broadcasted_iota(jnp.int32, (order, order), 0)
    col_ids = lax.broadcasted_iota(jnp.int32, (order, order), 1)
    return jnp.where(row_ids > col_ids, matrix, jnp.where(row_ids == col_ids, 0.5 * matrix, 0.0))


def cholesky_adjoint(factor, inverse, gradient):
    inner = halve_diagonal(product(factor.T, gradient))
    middle = product(product(inverse.T, inner), inverse)
    return halve_diagonal(middle + middle.T)


def per_device(trail_grad, factor_rows, factor_top, rows_grad, top_grad):
    row_owner = lax.axis_index("row")
    col_owner = lax.axis_index("col")
    row_owners = lax.axis_size("row")
    col_owners = lax.axis_size("col")
    owned_rows = trail_grad.shape[0]
    tiles_row = owned_rows // CB
    tiles_col = trail_grad.shape[1] // CB
    panel_width = NP * NB
    piece_rows = rows_grad.shape[0]
    panels = lax.all_gather(factor_rows, "row", axis=1, tiled=True)
    global_rows = (
        lax.broadcasted_iota(jnp.int32, (tiles_row, tiles_col), 0) * row_owners + row_owner
    )
    global_cols = (
        lax.broadcasted_iota(jnp.int32, (tiles_row, tiles_col), 1) * col_owners + col_owner
    )
    intersection = (global_rows == global_cols).astype(jnp.float32)
    aligned_rows = jnp.einsum(
        "kq,qtw->ktw",
        intersection,
        panels.reshape(tiles_col, CB, panel_width),
        precision=exact_dots,
        preferred_element_type=jnp.float32,
    ).reshape(owned_rows, panel_width)
    cross_factor = lax.psum_scatter(aligned_rows, "col", scatter_dimension=0, tiled=True)
    row_index = lax.broadcasted_iota(jnp.int32, (panel_width, NB), 0)
    identity = jnp.eye(NB, dtype=jnp.float32)
    adj_here = jnp.zeros((piece_rows, panel_width), jnp.float32)
    adj_top = jnp.zeros((panel_width, panel_width), jnp.float32)
    cross_adjoints = [None] * NP
    for which_panel in reversed(range(NP)):
        col_start = which_panel * NB
        col_end = col_start + NB
        below_diag = jnp.where(row_index >= col_end, factor_top[:, col_start:col_end], 0.0)
        diag_block = factor_top[col_start:col_end, col_start:col_end]
        inverse = jax.scipy.linalg.solve_triangular(diag_block, identity, lower=True)
        partial_rows = product(trail_grad, panels[:, col_start:col_end])
        summed_rows = lax.psum_scatter(partial_rows, "col", scatter_dimension=0, tiled=True)
        rows_cbar = (
            rows_grad[:, col_start:col_end] - 2.0 * summed_rows - product(adj_here, below_diag)
        )
        later_blocks = []
        if which_panel < NP - 1:
            cross_terms = jnp.stack(
                [
                    column_products(cross_adjoints[later_panel], cross_factor[:, col_start:col_end])
                    for later_panel in range(which_panel + 1, NP)
                ]
            )
            cross_summed = lax.psum(cross_terms, ("row", "col"))
            later_blocks = [
                cross_summed[later_panel - which_panel - 1]
                for later_panel in range(which_panel + 1, NP)
            ]
        if later_blocks:
            cross_part = jnp.concatenate([jnp.zeros((col_end, NB), jnp.float32)] + later_blocks, 0)
        else:
            cross_part = jnp.zeros((panel_width, NB), jnp.float32)
        top_masked = jnp.where(row_index >= col_end, top_grad[:, col_start:col_end], 0.0)
        top_cbar = top_masked - (product(adj_top + adj_top.T, below_diag) + cross_part)
        rows_adj = product(rows_cbar, inverse)
        top_adj = product(top_cbar, inverse)
        diag_sum = lax.psum(
            column_products(rows_adj, cross_factor[:, col_start:col_end]), ("row", "col")
        )
        diag_grad = jnp.tril(
            top_grad[col_start:col_end, col_start:col_end]
            - product(top_adj.T, below_diag)
            - diag_sum
        )
        diag_adjoint = cholesky_adjoint(diag_block, inverse, diag_grad)
        cross_adjoints[which_panel] = rows_adj
        adj_here = adj_here.at[:, col_start:col_end].set(rows_adj)
        adj_top = adj_top.at[:, col_start:col_end].set(
            top_adj.at[col_start:col_end].set(diag_adjoint)
        )
    return (adj_here, adj_top)


def solution(mesh):
    placed = (P("row", "col"), P("col", "row"), P(), P(("row", "col"), None), P())
    return jax.shard_map(
        per_device,
        mesh=mesh,
        in_specs=placed,
        out_specs=(P(("row", "col"), None), P()),
        check_vma=False,
    )
```

profile of v0, /device:TPU:97, one launch (start us, length us, event | category | flops | bytes accessed | tf_op | source)
XLA Modules:
  0.0 638.5 jit_solution(12279739426921874140)
XLA Ops:
  7.9 56.5 %all-gather.2.cloned.1.call-done = f32[1024,768]{0,1:T(8,128)} async-done(((f32[1024,48]{0,1:T(8,128)}), f32[1024,768]{0,1:T(8,128)}) %all-gather.2.cloned.1.call-update) | async-done | bytes 3145744 | tf_op jit(solution)/shard_map/all_gather | solution.py:45
  64.5 7.1 %fusion.16 = f32[1024,256]{1,0:T(8,128)} fusion(f32[1024,1024]{1,0:T(8,128)} %param.25, f32[1024,768]{0,1:T(8,128)} %all-gather.2.cloned.1.call-done), kind=kOutput, calls=%fused_computation.40 | convolution fusion | flops 3221225472 | bytes 6291456 | tf_op jit(solution)/shard_map/dot_general | solution.py:13
  71.6 6.6 %fusion.14 = f32[1024,256]{1,0:T(8,128)} fusion(f32[1024,1024]{1,0:T(8,128)} %param.25, f32[1024,768]{0,1:T(8,128)S(1)} %copy-done.2), kind=kOutput, calls=%fused_computation.38 | convolution fusion | flops 3221225472 | bytes 6291456 | tf_op jit(solution)/shard_map/dot_general | solution.py:13
  78.3 6.6 %fusion.12 = f32[1024,256]{1,0:T(8,128)} fusion(f32[1024,1024]{1,0:T(8,128)} %param.25, f32[1024,768]{0,1:T(8,128)S(1)} %copy-done.2), kind=kOutput, calls=%fused_computation.36 | convolution fusion | flops 3221225472 | bytes 6291456 | tf_op jit(solution)/shard_map/dot_general | solution.py:13
  85.2 2.4 copy.50
  87.6 3.3 fusion
  90.9 2.6 copy.52
  95.4 3.8 while.15
  99.1 19.7 %custom-call.5 = f32[2,128,128]{1,2,0:T(8,128)S(1)} custom-call(f32[2,128,128]{2,1,0:T(8,128)S(1)} %get-tuple-element.131), custom_call_target="InvertDiagBlocksLowerTriangular" | custom-call | tf_op jit(solution)/shard_map/jit(_solve_triangular)/triangular_solve | solution.py:71
  118.8 3.8 while.16
  122.7 20.3 %custom-call.6 = f32[2,128,128]{1,2,0:T(8,128)} custom-call(f32[2,128,128]{2,1,0:T(8,128)S(1)} %get-tuple-element.132), custom_call_target="InvertDiagBlocksLowerTriangular" | custom-call | tf_op jit(solution)/shard_map/jit(_solve_triangular)/triangular_solve | solution.py:71
  143.0 3.7 while.17
  146.7 20.3 %custom-call.7 = f32[2,128,128]{1,2,0:T(8,128)} custom-call(f32[2,128,128]{2,1,0:T(8,128)S(1)} %get-tuple-element.133), custom_call_target="InvertDiagBlocksLowerTriangular" | custom-call | tf_op jit(solution)/shard_map/jit(_solve_triangular)/triangular_solve | solution.py:71
  175.9 13.4 %reduce-scatter.7.cloned.1.call-done = f32[64,256]{1,0:T(8,128)} async-done(((f32[1024,256]{1,0:T(8,128)}), f32[64,256]{1,0:T(8,128)}) %reduce-scatter.7.cloned.1.call-update) | async-done | bytes 65552 | tf_op jit(solution)/shard_map/reduce_scatter | solution.py:73
  191.7 56.6 %reduce-scatter.9.cloned.1.call-done = f32[64,256]{1,0:T(8,128)} async-done(((f32[1024,256]{1,0:T(8,128)}), f32[64,256]{1,0:T(8,128)}) %reduce-scatter.9.cloned.1.call-update) | async-done | bytes 65552 | tf_op jit(solution)/shard_map/reduce_scatter | solution.py:73
  250.7 60.2 %reduce-scatter.11.cloned.1.call-done = f32[64,768]{1,0:T(8,128)} async-done(((f32[1024,768]{1,0:T(8,128)}), f32[64,768]{1,0:T(8,128)}) %reduce-scatter.11.cloned.1.call-update) | async-done | bytes 196624 | tf_op jit(solution)/shard_map/reduce_scatter | solution.py:60
  316.2 2.0 fusion.96
  320.6 2.0 fusion.22
  322.6 261.0 %all-reduce.6.cloned.1.call-done = (f32[256,256]{1,0:T(8,128)}, f32[256,256]{1,0:T(8,128)}, f32[256,256]{1,0:T(8,128)}, f32[2,256,256]{2,1,0:T(8,128)}, f32[256,256]{1,0:T(8,128)}) async-done(((f32[256,256]{1,0:T(8,128)}, f32[256,256]{1,0:T(8,128)}, f32[256,256]{1,0:T(8,128)}, f32[2,256,256]{2,1,0:T(8,128)}, f32[256,256]{1,0:T(8,128)}), (f32[256,256]{1,0:T(8,128)}, f32[256,256]{1,0:T(8,128)}, ...) | async-done | bytes 1572880 | tf_op jit(solution)/shard_map/psum | solution.py:98
  583.7 2.6 fusion.9
  592.5 3.5 fusion.5
  596.8 2.5 fusion.10
  609.8 6.2 fusion.4
  617.9 2.8 fusion.11
  (132 shorter events, 65.2 us)
Async XLA Ops:
  7.2 57.3 %all-gather.2.cloned.1.call-start = ((), (), s32[]{:S(2)}) async-start(), calls=%async_computation.4 | async-start | bytes 3342336 | tf_op jit(solution)/shard_map/all_gather | solution.py:45
  7.9 166.2 %reduce-scatter.5.cloned.1.call-start = ((), (), s32[]{:S(2)}) async-start(), calls=%async_computation.5 | async-start | bytes 1114112 | tf_op jit(solution)/shard_map/reduce_scatter | solution.py:73
  64.5 7.1 %copy-start.2 = (f32[1024,768]{0,1:T(8,128)S(1)}, f32[1024,768]{0,1:T(8,128)}, u32[]{:S(2)}) copy-start(f32[1024,768]{0,1:T(8,128)} %all-gather.2.cloned.1.call-done) | copy-start | bytes 9437188
  71.6 117.7 %reduce-scatter.7.cloned.1.call-start = ((), (), s32[]{:S(2)}) async-start(), calls=%async_computation.6 | async-start | bytes 1114112 | tf_op jit(solution)/shard_map/reduce_scatter | solution.py:73
  78.3 170.0 %reduce-scatter.9.cloned.1.call-start = ((), (), s32[]{:S(2)}) async-start(), calls=%async_computation.7 | async-start | bytes 1114112 | tf_op jit(solution)/shard_map/reduce_scatter | solution.py:73
  85.0 225.9 %reduce-scatter.11.cloned.1.call-start = ((), (), s32[]{:S(2)}) async-start(), calls=%async_computation.8 | async-start | bytes 3342336 | tf_op jit(solution)/shard_map/reduce_scatter | solution.py:60
  93.5 1.7 copy-start
  93.6 490.1 %all-reduce.6.cloned.1.call-start = ((), (), s32[]{:S(2)}) async-start(), calls=%async_computation.9 | async-start | bytes 3145728 | tf_op jit(solution)/shard_map/psum | solution.py:98
  122.7 46.0 %copy-start.11 = (f32[256,256]{1,0:T(8,128)}, f32[256,256]{1,0:T(8,128)S(1)}, u32[]{:S(2)}) copy-start(f32[256,256]{1,0:T(8,128)S(1)} %get-tuple-element.347) | copy-start | bytes 786436
  167.0 6.1 copy-start.16
  169.6 21.2 %copy-start.8 = (f32[128,256]{1,0:T(8,128)}, f32[128,256]{1,0:T(8,128)S(1)}, u32[]{:S(2)}) copy-start(f32[128,256]{1,0:T(8,128)S(1)} %fusion.93) | copy-start | bytes 393220
  173.1 76.7 %copy-start.6 = (f32[128,256]{1,0:T(8,128)}, f32[128,256]{1,0:T(8,128)S(1)}, u32[]{:S(2)}) copy-start(f32[128,256]{1,0:T(8,128)S(1)} %fusion.91) | copy-start | bytes 393220
  174.0 76.7 %copy-start.4 = (f32[128,256]{1,0:T(8,128)}, f32[128,256]{1,0:T(8,128)S(1)}, u32[]{:S(2)}) copy-start(f32[128,256]{1,0:T(8,128)S(1)} %fusion.89) | copy-start | bytes 393220
  250.7 69.8 %copy-start.12 = (f32[64,768]{1,0:T(8,128)}, f32[64,768]{1,0:T(8,128)S(1)}, u32[]{:S(2)}) copy-start(f32[64,768]{1,0:T(8,128)S(1)} %get-tuple-element.184) | copy-start | bytes 589828
  310.9 7.3 %copy-start.13 = (f32[64,768]{1,0:T(8,128)S(1)}, f32[64,768]{1,0:T(8,128)}, u32[]{:S(2)}) copy-start(f32[64,768]{1,0:T(8,128)} %reduce-scatter.11.cloned.1.call-done) | copy-start | bytes 589828
  583.7 3.2 copy-start.9
  589.3 1.5 copy-start.3
  589.3 1.6 copy-start.15
  590.8 1.7 copy-start.1
  592.5 3.5 copy-start.7
  592.5 4.3 copy-start.14
  609.8 6.2 copy-start.5
  620.8 7.0 %copy-start.10 = (f32[768,256]{0,1:T(8,128)S(1)}, f32[768,256]{0,1:T(8,128)}, u32[]{:S(2)}) copy-start(f32[768,256]{0,1:T(8,128)} %copy.62) | copy-start | bytes 2359300
Sparse Core Ops, SparseCore 0:
  10.4 54.0 all-gather.1
  71.7 58.0 reduce-scatter.4
  132.3 56.9 reduce-scatter.6
  191.7 56.5 reduce-scatter.8
  250.7 60.1 reduce-scatter.10
  320.6 263.0 all-reduce.5
where the time goes:
time: 648 us; the launch traced here: 638 us
  waiting for transfers between devices  449 us (69%)
  matrix products  72.5 us (11%)
  other arithmetic  67.5 us (10%)
  local copies, waits for them, and re-layouts  34.5 us (5%)
  between operations  14.9 us (2%)
    psum x1, waiting for transfers between devices, per_device(): lax.psum(column_products(rows_adj, cross_factor[:, col_start:col_end]), (...  261 us
    reduce_scatter x3, waiting for transfers between devices, per_device(): lax.psum_scatter(partial_rows, 'col', scatter_dimension=0, tiled=True)  70 us
    another operation x5, other arithmetic, per_device(): jax.scipy.linalg.solve_triangular(diag_block, identity, lower=True)  60.3 us
    reduce_scatter x1, waiting for transfers between devices, per_device(): lax.psum_scatter(aligned_rows, 'col', scatter_dimension=0, tiled=True)  60.2 us
    all_gather x1, waiting for transfers between devices, per_device(): panels = lax.all_gather(factor_rows, 'row', axis=1, tiled=True)  56.5 us
    dot_general x26, matrix products, product(): jnp.dot(left, right, precision=exact_dots, preferred_element_type=jnp.flo...  55.2 us
  transfers between devices with their start and end apart: 6, of which 5 were waited for; matrix products, arithmetic and copies ran while one was open for 17% of the time, Pallas kernels for 0%

commit v1 on v0

--- a/solution.py
+++ b/solution.py
@@ -95,9 +95,9 @@
         top_cbar = top_masked - (product(adj_top + adj_top.T, below_diag) + cross_part)
         rows_adj = product(rows_cbar, inverse)
         top_adj = product(top_cbar, inverse)
-        diag_sum = lax.psum(
-            column_products(rows_adj, cross_factor[:, col_start:col_end]), ("row", "col")
-        )
+        diag_sum = column_products(rows_adj, cross_factor[:, col_start:col_end])
+        for mesh_axis in ("row", "col"):
+            diag_sum = lax.psum(diag_sum, mesh_axis)
         diag_grad = jnp.tril(
             top_grad[col_start:col_end, col_start:col_end]
             - product(top_adj.T, below_diag)

time: 648 us -> 854 us (1.32)
  waiting for transfers between devices: 449 us -> 649 us
    psum x1 -> x3, waiting for transfers between devices: 261 us -> 462 us  [the longest x1 263 us: per_device(): cross_summed = lax.psum(cross_terms, ('row', 'col'))]
  transfers between devices with their start and end apart: 6 -> 8, of which waited for: 5 -> 7; matrix products, arithmetic and copies ran while one was open for 17% -> 14% of each run, Pallas kernels for 0% -> 0%
where the time goes in v1:
time: 854 us; the launch traced here: 843 us
  waiting for transfers between devices  649 us (76%)
  matrix products  74.1 us (9%)
  other arithmetic  67.4 us (8%)
  local copies, waits for them, and re-layouts  36.3 us (4%)
  between operations  15 us (2%)
    psum x1, waiting for transfers between devices, per_device(): cross_summed = lax.psum(cross_terms, ('row', 'col'))  263 us
    psum x2, waiting for transfers between devices, per_device(): diag_sum = lax.psum(diag_sum, mesh_axis)  199 us
    reduce_scatter x3, waiting for transfers between devices, per_device(): lax.psum_scatter(partial_rows, 'col', scatter_dimension=0, tiled=True)  69.4 us
    another operation x5, other arithmetic, per_device(): jax.scipy.linalg.solve_triangular(diag_block, identity, lower=True)  60.3 us
    reduce_scatter x1, waiting for transfers between devices, per_device(): lax.psum_scatter(aligned_rows, 'col', scatter_dimension=0, tiled=True)  60.3 us
    all_gather x1, waiting for transfers between devices, per_device(): panels = lax.all_gather(factor_rows, 'row', axis=1, tiled=True)  56.5 us
    dot_general x26, matrix products, product(): jnp.dot(left, right, precision=exact_dots, preferred_element_type=jnp.flo...  55.2 us
  transfers between devices with their start and end apart: 8, of which 7 were waited for; matrix products, arithmetic and copies ran while one was open for 14% of the time, Pallas kernels for 0%

profile of v1, /device:TPU:97, one launch (start us, length us, event | category | flops | bytes accessed | tf_op | source)
XLA Modules:
  0.0 842.7 jit_solution(18171401651975525231)
XLA Ops:
  7.9 56.5 %all-gather.2.cloned.1.call-done = f32[1024,768]{0,1:T(8,128)} async-done(((f32[1024,48]{0,1:T(8,128)}), f32[1024,768]{0,1:T(8,128)}) %all-gather.2.cloned.1.call-update) | async-done | bytes 3145744 | tf_op jit(solution)/shard_map/all_gather | solution.py:45
  64.5 7.1 fusion.16
  71.6 6.6 fusion.14
  78.3 6.6 fusion.12
  85.2 2.4 copy.50
  87.6 3.3 fusion
  90.9 2.6 copy.52
  95.4 4.1 while.15
  99.5 19.7 %custom-call.5 = f32[2,128,128]{1,2,0:T(8,128)S(1)} custom-call(f32[2,128,128]{2,1,0:T(8,128)S(1)} %get-tuple-element.131), custom_call_target="InvertDiagBlocksLowerTriangular" | custom-call | tf_op jit(solution)/shard_map/jit(_solve_triangular)/triangular_solve | solution.py:71
  119.2 4.0 while.16
  123.2 20.3 %custom-call.6 = f32[2,128,128]{1,2,0:T(8,128)} custom-call(f32[2,128,128]{2,1,0:T(8,128)S(1)} %get-tuple-element.132), custom_call_target="InvertDiagBlocksLowerTriangular" | custom-call | tf_op jit(solution)/shard_map/jit(_solve_triangular)/triangular_solve | solution.py:71
  143.5 4.0 while.17
  147.5 20.3 %custom-call.7 = f32[2,128,128]{1,2,0:T(8,128)} custom-call(f32[2,128,128]{2,1,0:T(8,128)S(1)} %get-tuple-element.133), custom_call_target="InvertDiagBlocksLowerTriangular" | custom-call | tf_op jit(solution)/shard_map/jit(_solve_triangular)/triangular_solve | solution.py:71
  176.4 12.8 %reduce-scatter.7.cloned.1.call-done = f32[64,256]{1,0:T(8,128)} async-done(((f32[1024,256]{1,0:T(8,128)}), f32[64,256]{1,0:T(8,128)}) %reduce-scatter.7.cloned.1.call-update) | async-done | bytes 65552 | tf_op jit(solution)/shard_map/reduce_scatter | solution.py:73
  191.7 56.6 %reduce-scatter.9.cloned.1.call-done = f32[64,256]{1,0:T(8,128)} async-done(((f32[1024,256]{1,0:T(8,128)}), f32[64,256]{1,0:T(8,128)}) %reduce-scatter.9.cloned.1.call-update) | async-done | bytes 65552 | tf_op jit(solution)/shard_map/reduce_scatter | solution.py:73
  250.8 60.3 %reduce-scatter.11.cloned.1.call-done = f32[64,768]{1,0:T(8,128)} async-done(((f32[1024,768]{1,0:T(8,128)}), f32[64,768]{1,0:T(8,128)}) %reduce-scatter.11.cloned.1.call-update) | async-done | bytes 196624 | tf_op jit(solution)/shard_map/reduce_scatter | solution.py:60
  323.0 88.2 %all-reduce.14.cloned.1.call-done = (f32[256,256]{1,0:T(8,128)}, f32[256,256]{1,0:T(8,128)}, f32[256,256]{1,0:T(8,128)}) async-done(((f32[256,256]{1,0:T(8,128)}, f32[256,256]{1,0:T(8,128)}, f32[256,256]{1,0:T(8,128)}), (f32[256,256]{1,0:T(8,128)}, f32[256,256]{1,0:T(8,128)}, f32[256,256]{1,0:T(8,128)})) %all-reduce.14.cloned.1.call-update) | async-done | bytes 786448 | tf_op jit(solution)/shard_map/psum | solution.py:100
  413.3 263.3 %all-reduce.10.cloned.1.call-done = (f32[256,256]{1,0:T(8,128)}, f32[2,256,256]{2,1,0:T(8,128)}) async-done(((f32[256,256]{1,0:T(8,128)}, f32[2,256,256]{2,1,0:T(8,128)}), (f32[256,256]{1,0:T(8,128)}, f32[2,256,256]{2,1,0:T(8,128)})) %all-reduce.10.cloned.1.call-update) | async-done | bytes 786448 | tf_op jit(solution)/shard_map/psum | solution.py:85
  678.4 110.4 %all-reduce.12.cloned.1.call-done = (f32[256,256]{1,0:T(8,128)}, f32[256,256]{1,0:T(8,128)}, f32[256,256]{1,0:T(8,128)}) async-done(((f32[256,256]{1,0:T(8,128)}, f32[256,256]{1,0:T(8,128)}, f32[256,256]{1,0:T(8,128)}), (f32[256,256]{1,0:T(8,128)}, f32[256,256]{1,0:T(8,128)}, f32[256,256]{1,0:T(8,128)})) %all-reduce.12.cloned.1.call-update) | async-done | bytes 786448 | tf_op jit(solution)/shard_map/psum | solution.py:100
  788.8 2.6 fusion.9
  797.6 3.3 fusion.5
  801.7 2.5 fusion.10
  813.9 6.2 fusion.4
  822.1 2.8 fusion.11
  (140 shorter events, 73.1 us)
Async XLA Ops:
  7.2 57.3 %all-gather.2.cloned.1.call-start = ((), (), s32[]{:S(2)}) async-start(), calls=%async_computation.4 | async-start | bytes 3342336 | tf_op jit(solution)/shard_map/all_gather | solution.py:45
  7.9 166.7 %reduce-scatter.5.cloned.1.call-start = ((), (), s32[]{:S(2)}) async-start(), calls=%async_computation.5 | async-start | bytes 1114112 | tf_op jit(solution)/shard_map/reduce_scatter | solution.py:73
  64.5 7.1 copy-start.2
  71.6 117.7 %reduce-scatter.7.cloned.1.call-start = ((), (), s32[]{:S(2)}) async-start(), calls=%async_computation.6 | async-start | bytes 1114112 | tf_op jit(solution)/shard_map/reduce_scatter | solution.py:73
  78.3 170.0 %reduce-scatter.9.cloned.1.call-start = ((), (), s32[]{:S(2)}) async-start(), calls=%async_computation.7 | async-start | bytes 1114112 | tf_op jit(solution)/shard_map/reduce_scatter | solution.py:73
  85.0 226.1 %reduce-scatter.11.cloned.1.call-start = ((), (), s32[]{:S(2)}) async-start(), calls=%async_computation.8 | async-start | bytes 3342336 | tf_op jit(solution)/shard_map/reduce_scatter | solution.py:60
  93.5 1.7 copy-start
  93.6 317.7 %all-reduce.14.cloned.1.call-start = ((), (), s32[]{:S(2)}) async-start(), calls=%async_computation.11 | async-start | bytes 1572864 | tf_op jit(solution)/shard_map/psum | solution.py:100
  123.1 46.1 %copy-start.11 = (f32[256,256]{1,0:T(8,128)}, f32[256,256]{1,0:T(8,128)S(1)}, u32[]{:S(2)}) copy-start(f32[256,256]{1,0:T(8,128)S(1)} %get-tuple-element.356) | copy-start | bytes 786436
  167.8 5.9 copy-start.17
  170.1 20.6 %copy-start.8 = (f32[128,256]{1,0:T(8,128)}, f32[128,256]{1,0:T(8,128)S(1)}, u32[]{:S(2)}) copy-start(f32[128,256]{1,0:T(8,128)S(1)} %fusion.93) | copy-start | bytes 393220
  173.6 76.2 %copy-start.6 = (f32[128,256]{1,0:T(8,128)}, f32[128,256]{1,0:T(8,128)S(1)}, u32[]{:S(2)}) copy-start(f32[128,256]{1,0:T(8,128)S(1)} %fusion.91) | copy-start | bytes 393220
  174.5 76.2 %copy-start.4 = (f32[128,256]{1,0:T(8,128)}, f32[128,256]{1,0:T(8,128)S(1)}, u32[]{:S(2)}) copy-start(f32[128,256]{1,0:T(8,128)S(1)} %fusion.89) | copy-start | bytes 393220
  250.8 72.0 %copy-start.12 = (f32[64,768]{1,0:T(8,128)}, f32[64,768]{1,0:T(8,128)S(1)}, u32[]{:S(2)}) copy-start(f32[64,768]{1,0:T(8,128)S(1)} %get-tuple-element.187) | copy-start | bytes 589828
  317.0 359.5 %all-reduce.10.cloned.1.call-start = ((), (), s32[]{:S(2)}) async-start(), calls=%async_computation.9 | async-start | bytes 1572864 | tf_op jit(solution)/shard_map/psum | solution.py:85
  322.8 466.0 %all-reduce.12.cloned.1.call-start = ((), (), s32[]{:S(2)}) async-start(), calls=%async_computation.10 | async-start | bytes 1572864 | tf_op jit(solution)/shard_map/psum | solution.py:100
  788.8 3.2 copy-start.9
  795.9 1.7 copy-start.1
  797.6 3.3 copy-start.7
  797.6 4.1 copy-start.15
  811.7 2.2 copy-start.13
  811.7 2.2 copy-start.14
  813.9 6.2 copy-start.5
  824.9 7.0 copy-start.10
  (2 other events, 3.2 us)
Sparse Core Ops, SparseCore 0:
  10.4 54.0 all-gather.1
  71.7 57.9 reduce-scatter.4
  132.2 56.9 reduce-scatter.6
  191.6 56.6 reduce-scatter.8
  250.7 60.3 reduce-scatter.10
  317.1 94.0 all-reduce.13
  417.5 258.9 all-reduce.9
  679.0 109.7 all-reduce.11
